TPU v7x, 32 devices: a whole 2x2x4 slice. The times are simulated.
32 devices in a mesh: brick: 8 (over y, x, core), kvec: 4 (over z).
Axes of the slice: x: 2, y: 2, z: 4, core: 2. Of those that a mesh axis runs over, the one named last changes fastest.
Arguments:
- positions: float32 [2, 3, 1024], P(None, None, 'brick'), may hold values from -20 to 20
- moments: float32 [1024, 640], P('brick'), may hold values from -4 to 4
- adj_pos: float32 [3, 1024], P(None, 'brick'), may hold values from -1.8 to 1.8
- final_momentum_adjoint: float32 [3, 1024], P(None, 'brick'), may hold values from -6 to 6
- species: int32 [1024], P('brick'), may hold values from 0 to 5
- masses: float32 [6], replicated, may hold values from 1 to 16
- kint: int32 [1536, 3], P('kvec'), may hold values from -5 to 5
Outputs:
- pos_adjoint: float32 [3, 1024], P(None, 'brick')
- initial_momentum_adjoint: float32 [3, 1024], P(None, 'brick')
All inputs are finite; a program needn't handle non-finite values.
Results may differ from a plain program's by a relative error of at most 0.0003.
Values sent between devices are 32-bit elements; how exact they have to be, the bound alone decides.
A program may use at most 64 MiB of HBM per device.

v0:
```python
import math

import jax
import jax.numpy as jnp
from jax import lax
from jax.sharding import PartitionSpec as P

exact = lax.Precision.HIGHEST
wavevector_scale = 0.5
time_step = 0.5
energy_scale = 0.125


def coef_arrays(wavevector_phase):
    kx, ky, kz = (wavevector_phase[:, 0], wavevector_phase[:, 1], wavevector_phase[:, 2])
    ones = jnp.ones_like(kx)
    zeros = jnp.zeros_like(kx)
    acoef = jnp.stack(
        [
            ones,
            zeros,
            zeros,
            zeros,
            -0.5 * kx * kx,
            -0.5 * ky * ky,
            -0.5 * kz * kz,
            -kx * ky,
            -kx * kz,
            -ky * kz,
        ],
        1,
    )
    bcoef = jnp.stack([zeros, kx, ky, kz, zeros, zeros, zeros, zeros, zeros, zeros], 1)
    return (acoef, bcoef)


def moment_sums(cos_w, sin_w, moments, acoef, bcoef):
    channels = moments.shape[1] // 10
    cos_part = jnp.dot(cos_w, moments, precision=exact).reshape(cos_w.shape[0], 10, channels)
    sine_component = jnp.dot(sin_w, moments, precision=exact).reshape(cos_w.shape[0], 10, channels)
    real_sum = jnp.einsum("km,kmc->kc", acoef, cos_part, precision=exact) - jnp.einsum(
        "km,kmc->kc", bcoef, sine_component, precision=exact
    )
    imag_sum = jnp.einsum("km,kmc->kc", acoef, sine_component, precision=exact) + jnp.einsum(
        "km,kmc->kc", bcoef, cos_part, precision=exact
    )
    return (real_sum, imag_sum)


def weave_terms(leading_dimension, trailing, acoef, bcoef):
    woven = (
        leading_dimension[:, None, :] * acoef[:, :, None] + trailing[:, None, :] * bcoef[:, :, None]
    )
    return woven.reshape(leading_dimension.shape[0], -1)


def tangent_force(
    wavevector_phase,
    k_weight,
    acoef,
    bcoef,
    factor,
    tangent,
    cosines,
    sines,
    k_dot_dir,
    moments,
    prefactor,
):
    factor_re, factor_im = factor
    tangent_re, tangent_im = tangent
    stacked = jnp.stack(
        [
            weave_terms(tangent_im, -tangent_re, acoef, bcoef),
            weave_terms(tangent_re, tangent_im, acoef, bcoef),
            weave_terms(factor_re, factor_im, acoef, bcoef),
            weave_terms(factor_im, -factor_re, acoef, bcoef),
        ]
    )
    projected = jnp.einsum("jkf,af->jka", stacked, moments, precision=exact)
    inner_sum = (
        cosines * projected[0]
        - sines * projected[1]
        - k_dot_dir * (cosines * projected[2] + sines * projected[3])
    )
    return jnp.dot((k_weight[:, None] * wavevector_phase).T, inner_sum, precision=exact) * prefactor


def local(positions, moments, adj_pos, final_momentum_adjoint, species, masses, kint):
    wavevector_phase = kint.astype(jnp.float32) * wavevector_scale
    ksq = jnp.sum(wavevector_phase * wavevector_phase, 1)
    k_weight = jnp.exp(-ksq / 4.0) / jnp.maximum(ksq, 1.0)
    acoef, bcoef = coef_arrays(wavevector_phase)
    prefactor = energy_scale / math.sqrt(positions.shape[2] * lax.axis_size("brick"))
    onehot = (species[None, :] == jnp.arange(masses.shape[0], dtype=jnp.int32)[:, None]).astype(
        jnp.float32
    )
    inv_mass = jnp.dot(1.0 / masses, onehot, precision=exact)
    num_steps = positions.shape[0]

    def step_phases(step_index):
        phase = jnp.dot(wavevector_phase, positions[step_index], precision=exact)
        return (jnp.cos(phase), jnp.sin(phase))

    phase_list = [step_phases(step_index) for step_index in range(num_steps)]
    for step_index in reversed(range(num_steps)):
        cosines, sines = phase_list[step_index]
        direction = final_momentum_adjoint * inv_mass
        k_dot_dir = jnp.dot(wavevector_phase, direction, precision=exact)
        tangent_real_part, tan_im = moment_sums(
            k_dot_dir * cosines, k_dot_dir * sines, moments, acoef, bcoef
        )
        fac_re, fac_im = moment_sums(cosines, sines, moments, acoef, bcoef)
        summed_terms = lax.psum((fac_re, fac_im, -tan_im, tangent_real_part), "brick")
        factor = (summed_terms[0], summed_terms[1])
        tangent = (summed_terms[2], summed_terms[3])
        partial_force = tangent_force(
            wavevector_phase,
            k_weight,
            acoef,
            bcoef,
            factor,
            tangent,
            cosines,
            sines,
            k_dot_dir,
            moments,
            prefactor,
        )
        force = lax.psum(partial_force, "kvec")
        adj_pos = adj_pos - time_step * force
        final_momentum_adjoint = final_momentum_adjoint + time_step * adj_pos
    return (adj_pos, final_momentum_adjoint)


def solution(mesh):
    placed = (
        P(None, None, "brick"),
        P("brick", None),
        P(None, "brick"),
        P(None, "brick"),
        P("brick"),
        P(),
        P("kvec", None),
    )
    return jax.shard_map(
        local,
        mesh=mesh,
        in_specs=placed,
        out_specs=(P(None, "brick"), P(None, "brick")),
        check_vma=False,
    )
```

profile of v0, /device:TPU:0, one launch (start us, length us, event | category | flops | bytes accessed | tf_op | source)
XLA Modules:
  0.0 208.2 jit_solution(1347344306516138420)
XLA Ops:
  7.2 0.0 copy-start
  7.2 0.0 all-reduce.7.cloned.1.call-start
  7.2 0.8 fusion.74
  8.0 0.7 multiply_reduce_fusion.16
  8.7 1.8 fusion.72
  10.5 0.0 copy-start.4
  10.5 0.0 copy-start.6
  10.5 0.9 convolution_bitcast_fusion
  11.4 1.2 fusion.60
  12.7 1.0 fusion.75
  13.6 1.0 fusion.48
  14.6 1.0 fusion.76
  15.6 0.0 copy-start.20
  15.6 1.9 fusion.46
  17.5 0.6 negate_multiply_fusion
  18.1 1.1 fusion.73
  19.2 1.9 fusion.78
  21.2 2.0 fusion.77
  23.1 0.1 pad.11.clone
  23.2 0.1 maximum_maximum_fusion
  23.3 0.6 max.14
  23.9 1.4 stack.22
  25.2 3.6 %multiply_reduce_fusion.9 = (f32[384,64]{0,1:T(8,128)S(1)}, f32[384,64]{0,1:T(8,128)S(1)}, f32[384,64]{0,1:T(8,128)}, f32[384,64]{0,1:T(8,128)}, f32[384,64]{0,1...) fusion(f32[384,10,64]{0,2,1:T(8,128)S(1)} %bitcast.118, ...), kind=kLoop, calls=%fused_computation.28 | loop fusion | flops 5603328 | bytes 7108608 | tf_op jit(solution)/shard_map/km,kmc->kc/dot_general | solution.py:44
  28.8 0.6 add.153
  29.4 0.6 sub.31
  30.1 0.6 add_negate_fusion.1
  30.7 0.6 sub.30
  31.4 0.0 all-reduce.7.cloned.1.call-update
  31.4 0.2 all-reduce.5.cloned.1.call-start
  31.6 0.6 sub.36
  32.3 0.6 add.165
  32.9 55.7 %all-reduce.7.cloned.1.call-done = (f32[384,64]{0,1:T(8,128)}, f32[384,64]{0,1:T(8,128)}, f32[384,64]{0,1:T(8,128)}, f32[384,64]{0,1:T(8,128)}) async-done(((f32[384,64]{0,1:T(8,128)}, f32[384,64]{0,1:T(8,128)}, f32[384,64]{0,1:T(8,128)}, f32[384,64]{0,1:T(8,128)}), (f32[384,64]{0,1:T(8,128)}, f32[384,64]{0,1:T(8,128)}, f32[384,64]{0,1:T(8,128)}, f32[384,64]{0,1:T(8,128)})) %all-reduce.7.cloned.1.call-update) | async-done | bytes 393232 | tf_op jit(solution)/shard_map/psum | solution.py:114
  88.7 0.9 neg.40
  89.6 0.9 neg.39
  90.5 2.5 %multiply_add_fusion.7 = (f32[384,10,64]{0,2,1:T(8,128)}, f32[384,10,64]{0,2,1:T(8,128)S(1)}, f32[384,10,64]{0,2,1:T(8,128)S(1)}, f32[384,10,64]{0,2,1:T(8,128)S(1)}) fusion(f32[384,10]{0,1:T(8,128)S(1)} %maximum_maximum_fusion, f32[384,10]{0,1:T(8,128)S(1)} %stack.22, f32[384,64]{0,1:T(8,128)S(1)} %neg.39, f32[384,64]{0,1:T(8,128)} %get-tuple-element.37, ...), kind=kLoop, calls=%fused_computation.42 | loop fusion | flops 2949120 | bytes 4552704 | tf_op jit(solution)/shard_map/add | solution.py:52
  93.0 2.5 %copy.20 = f32[1,384,640]{2,1,0:T(8,128)} copy(f32[1,384,640]{1,2,0:T(8,128)} %bitcast.131) | data formatting | bytes 1966080 | tf_op jit(solution)/shard_map/add | solution.py:52
  95.5 1.3 copy.21
  96.8 1.3 copy.23
  98.1 1.3 copy.22
  99.4 0.5 copy-done.14
  100.0 0.0 copy-start.22
  100.0 5.1 %fusion = f32[4,384,128]{2,1,0:T(8,128)S(1)} fusion(f32[1,384,640]{2,1,0:T(8,128)} %copy.23, f32[1,384,640]{2,1,0:T(8,128)} %copy.22, f32[1,384,640]{2,1,0:T(8,128)S(1)} %copy-done.14, f32[1,384,640]{2,1,0:T(8,128)S(1)} %copy-done.12, f32[128,640]{1,0:T(8,128)S(1)} %copy-done), kind=kOutput, calls=%fused_computation | convolution fusion | flops 1512898560 | bytes 5046272 | tf_op jit(solution)/shard_map/jkf,af->jka/dot_general | solution.py:80
  105.1 0.3 convolution_multiply_fusion.1
  105.4 11.8 %psum.74 = f32[3,128]{1,0:T(4,128)S(1)} all-reduce(f32[3,128]{1,0:T(4,128)S(1)} %convolution_multiply_fusion.1), channel_id=1, replica_groups=mesh['brick'=8,'kvec'=4] {'kvec'}, use_global_device_ids=true, to_apply=%region_5.0 | all-reduce | flops 384 | bytes 3072 | tf_op jit(solution)/shard_map/psum | solution.py:130
  117.2 0.5 fusion.58
  117.7 1.0 fusion.42
  118.7 1.0 fusion.44
  119.7 0.3 multiply_reduce_fusion.7
  120.0 0.6 sub.35
  120.6 0.6 add_negate_fusion
  121.2 0.0 all-reduce.5.cloned.1.call-update
  121.3 51.2 %all-reduce.5.cloned.1.call-done = (f32[384,64]{0,1:T(8,128)}, f32[384,64]{0,1:T(8,128)}, f32[384,64]{0,1:T(8,128)}, f32[384,64]{0,1:T(8,128)}) async-done(((f32[384,64]{0,1:T(8,128)}, f32[384,64]{0,1:T(8,128)}, f32[384,64]{0,1:T(8,128)}, f32[384,64]{0,1:T(8,128)}), (f32[384,64]{0,1:T(8,128)}, f32[384,64]{0,1:T(8,128)}, f32[384,64]{0,1:T(8,128)}, f32[384,64]{0,1:T(8,128)})) %all-reduce.5.cloned.1.call-update) | async-done | bytes 393232 | tf_op jit(solution)/shard_map/psum | solution.py:114
  172.5 0.9 neg.43
  173.4 0.9 neg.42
  174.3 2.5 %multiply_add_fusion.3 = (f32[384,10,64]{0,2,1:T(8,128)}, f32[384,10,64]{0,2,1:T(8,128)S(1)}, f32[384,10,64]{0,2,1:T(8,128)S(1)}, f32[384,10,64]{0,2,1:T(8,128)S(1)}) fusion(f32[384,10]{0,1:T(8,128)S(1)} %maximum_maximum_fusion, f32[384,10]{0,1:T(8,128)S(1)} %stack.22, f32[384,64]{0,1:T(8,128)S(1)} %neg.42, f32[384,64]{0,1:T(8,128)} %get-tuple-element.33, ...), kind=kLoop, calls=%fused_computation.38 | loop fusion | flops 2949120 | bytes 4552704 | tf_op jit(solution)/shard_map/add | solution.py:52
  176.8 2.5 %copy.28 = f32[1,384,640]{2,1,0:T(8,128)} copy(f32[1,384,640]{1,2,0:T(8,128)} %bitcast.129) | data formatting | bytes 1966080 | tf_op jit(solution)/shard_map/add | solution.py:52
  179.3 1.3 copy.29
  180.6 1.3 copy.31
  181.9 1.3 copy.30
  183.2 0.5 copy-done.15
  183.7 5.0 %fusion.8 = f32[4,384,128]{2,1,0:T(8,128)S(1)} fusion(f32[1,384,640]{2,1,0:T(8,128)} %copy.31, f32[1,384,640]{2,1,0:T(8,128)} %copy.30, f32[1,384,640]{2,1,0:T(8,128)S(1)} %copy-done.15, f32[1,384,640]{2,1,0:T(8,128)S(1)} %copy-done.13, f32[128,640]{1,0:T(8,128)S(1)} %copy-done), kind=kOutput, calls=%fused_computation.8 | convolution fusion | flops 1512898560 | bytes 5046272 | tf_op jit(solution)/shard_map/jkf,af->jka/dot_general | solution.py:80
  188.8 0.3 convolution_multiply_fusion
  189.1 11.7 %psum.79 = f32[3,128]{1,0:T(4,128)S(1)} all-reduce(f32[3,128]{1,0:T(4,128)S(1)} %convolution_multiply_fusion), channel_id=1, replica_groups=mesh['brick'=8,'kvec'=4] {'kvec'}, use_global_device_ids=true, to_apply=%region_10.0 | all-reduce | flops 384 | bytes 3072 | tf_op jit(solution)/shard_map/psum | solution.py:130
  200.8 0.6 multiply_add_fusion.8
  (47 shorter events, 0.1 us)
Async XLA Ops:
  7.2 5.5 %copy-start = (f32[128,640]{1,0:T(8,128)S(1)}, f32[128,640]{1,0:T(8,128)}, u32[]{:S(2)}) copy-start(f32[128,640]{1,0:T(8,128)} %param.8) | copy-start | bytes 983044
  7.2 81.5 %all-reduce.7.cloned.1.call-start = ((), (), s32[]{:S(2)}) async-start(), calls=%async_computation.1 | async-start | bytes 786432 | tf_op jit(solution)/shard_map/psum | solution.py:114
  10.5 4.1 %copy-start.4 = (f32[384,128]{1,0:T(8,128)}, f32[384,128]{1,0:T(8,128)S(1)}, u32[]{:S(2)}) copy-start(f32[384,128]{1,0:T(8,128)S(1)} %get-tuple-element.40) | copy-start | bytes 589828
  10.5 5.1 %copy-start.6 = (f32[384,128]{1,0:T(8,128)}, f32[384,128]{1,0:T(8,128)S(1)}, u32[]{:S(2)}) copy-start(f32[384,128]{1,0:T(8,128)S(1)} %get-tuple-element.41) | copy-start | bytes 589828
  11.4 3.2 %copy-start.23 = (f32[128]{0:T(128)}, f32[128]{0:T(128)S(1)}, u32[]{:S(2)}) copy-start(f32[128]{0:T(128)S(1)} %convolution_bitcast_fusion) | copy-start | bytes 1540
  12.6 3.0 %copy-start.8 = (f32[384,128]{1,0:T(8,128)}, f32[384,128]{1,0:T(8,128)S(1)}, u32[]{:S(2)}) copy-start(f32[384,128]{1,0:T(8,128)S(1)} %fusion.60) | copy-start | bytes 589828
  15.6 2.5 %copy-start.20 = (s32[384,3]{0,1:T(4,128)S(1)}, s32[384,3]{0,1:T(4,128)}, u32[]{:S(2)}) copy-start(s32[384,3]{0,1:T(4,128)} %param.13) | copy-start | bytes 13828
  19.2 3.9 %copy-start.1 = (f32[384,128]{1,0:T(8,128)}, f32[384,128]{1,0:T(8,128)S(1)}, u32[]{:S(2)}) copy-start(f32[384,128]{1,0:T(8,128)S(1)} %get-tuple-element.43) | copy-start | bytes 589828
  28.8 2.8 %copy-start.18 = (f32[384,64]{0,1:T(8,128)S(1)}, f32[384,64]{0,1:T(8,128)}, u32[]{:S(2)}) copy-start(f32[384,64]{0,1:T(8,128)} %get-tuple-element.18) | copy-start | bytes 294916
  28.8 2.8 %copy-start.19 = (f32[384,64]{0,1:T(8,128)S(1)}, f32[384,64]{0,1:T(8,128)}, u32[]{:S(2)}) copy-start(f32[384,64]{0,1:T(8,128)} %get-tuple-element.20) | copy-start | bytes 294916
  28.8 3.5 %copy-start.16 = (f32[384,64]{0,1:T(8,128)S(1)}, f32[384,64]{0,1:T(8,128)}, u32[]{:S(2)}) copy-start(f32[384,64]{0,1:T(8,128)} %get-tuple-element.19) | copy-start | bytes 294916
  28.8 3.5 %copy-start.17 = (f32[384,64]{0,1:T(8,128)S(1)}, f32[384,64]{0,1:T(8,128)}, u32[]{:S(2)}) copy-start(f32[384,64]{0,1:T(8,128)} %get-tuple-element.21) | copy-start | bytes 294916
  31.4 141.1 %all-reduce.5.cloned.1.call-start = ((), (), s32[]{:S(2)}) async-start(), calls=%async_computation | async-start | bytes 786432 | tf_op jit(solution)/shard_map/psum | solution.py:114
  98.1 1.3 copy-start.12
  98.1 1.9 copy-start.14
  100.0 5.1 %copy-start.5 = (f32[384,128]{1,0:T(8,128)S(1)}, f32[384,128]{1,0:T(8,128)}, u32[]{:S(2)}) copy-start(f32[384,128]{1,0:T(8,128)} %copy-done.4) | copy-start | bytes 589828
  100.0 5.1 %copy-start.7 = (f32[384,128]{1,0:T(8,128)S(1)}, f32[384,128]{1,0:T(8,128)}, u32[]{:S(2)}) copy-start(f32[384,128]{1,0:T(8,128)} %copy-done.6) | copy-start | bytes 589828
  100.0 5.1 %copy-start.9 = (f32[384,128]{1,0:T(8,128)S(1)}, f32[384,128]{1,0:T(8,128)}, u32[]{:S(2)}) copy-start(f32[384,128]{1,0:T(8,128)} %copy-done.8) | copy-start | bytes 589828
  100.0 17.2 %copy-start.21 = (f32[3,128]{1,0:T(4,128)S(1)}, f32[3,128]{1,0:T(4,128)}, u32[]{:S(2)}) copy-start(f32[3,128]{1,0:T(4,128)} %param.10) | copy-start | bytes 4612
  100.0 17.2 %copy-start.22 = (f32[3,128]{1,0:T(4,128)S(1)}, f32[3,128]{1,0:T(4,128)}, u32[]{:S(2)}) copy-start(f32[3,128]{1,0:T(4,128)} %param.9) | copy-start | bytes 4612
  100.0 17.2 %copy-start.24 = (f32[128]{0:T(128)S(1)}, f32[128]{0:T(128)}, u32[]{:S(2)}) copy-start(f32[128]{0:T(128)} %copy-done.23) | copy-start | bytes 1540
  105.3 13.3 %copy-start.2 = (f32[384,128]{1,0:T(8,128)S(1)}, f32[384,128]{1,0:T(8,128)}, u32[]{:S(2)}) copy-start(f32[384,128]{1,0:T(8,128)} %copy-done.1) | copy-start | bytes 589828
  117.7 2.0 copy-start.10
  181.9 1.3 copy-start.13
  181.9 1.9 copy-start.15
  183.7 5.1 %copy-start.3 = (f32[384,128]{1,0:T(8,128)S(1)}, f32[384,128]{1,0:T(8,128)}, u32[]{:S(2)}) copy-start(f32[384,128]{1,0:T(8,128)} %copy-done.1) | copy-start | bytes 589828
  183.7 5.1 %copy-start.11 = (f32[384,128]{1,0:T(8,128)S(1)}, f32[384,128]{1,0:T(8,128)}, u32[]{:S(2)}) copy-start(f32[384,128]{1,0:T(8,128)} %copy-done.10) | copy-start | bytes 589828
Sparse Core Ops, SparseCore 0:
  31.5 57.1 all-reduce.6
  121.4 51.0 all-reduce.4
where the time goes:
time: 209 us; the launch traced here: 208 us
  waiting for transfers between devices  107 us (51%)
  matrix products  26.8 us (13%)
  blocking collectives  23.5 us (11%)
  other arithmetic  19.6 us (9%)
  local copies, waits for them, and re-layouts  16.8 us (8%)
  between operations  14.3 us (7%)
    psum x2, waiting for transfers between devices, local(): lax.psum((fac_re, fac_im, -tan_im, tangent_real_part), 'brick')  107 us
    psum x2, blocking collectives, local(): force = lax.psum(partial_force, 'kvec')  23.5 us
    add x8, local copies, waits for them, and re-layouts, weave_terms(): leading_dimension[:, None, :] * acoef[:, :, None]  12.8 us
    dot_general x2, matrix products, tangent_force(): projected = jnp.einsum('jkf,af->jka', stacked, moments, precision=exact)  10.1 us
    dot_general x4, matrix products, moment_sums(): jnp.dot(sin_w, moments, precision=exact)  5.79 us
    add x2, other arithmetic, weave_terms(): leading_dimension[:, None, :] * acoef[:, :, None]  5.07 us
    dot_general x4, matrix products, moment_sums(): jnp.dot(cos_w, moments, precision=exact)  4.85 us
  transfers between devices with their start and end apart: 2, of which 2 were waited for; matrix products, arithmetic and copies ran while one was open for 1% of the time, Pallas kernels for 0%

commit v1 on v0

--- a/solution.py
+++ b/solution.py
@@ -1,8 +1,11 @@
+import functools
 import math
 
 import jax
 import jax.numpy as jnp
 from jax import lax
+from jax.experimental import pallas as pl
+from jax.experimental.pallas import tpu as pltpu
 from jax.sharding import PartitionSpec as P
 
 exact = lax.Precision.HIGHEST
@@ -86,7 +89,7 @@
     return jnp.dot((k_weight[:, None] * wavevector_phase).T, inner_sum, precision=exact) * prefactor
 
 
-def local(positions, moments, adj_pos, final_momentum_adjoint, species, masses, kint):
+def plain_local(positions, moments, adj_pos, final_momentum_adjoint, species, masses, kint):
     wavevector_phase = kint.astype(jnp.float32) * wavevector_scale
     ksq = jnp.sum(wavevector_phase * wavevector_phase, 1)
     k_weight = jnp.exp(-ksq / 4.0) / jnp.maximum(ksq, 1.0)
@@ -133,7 +136,7 @@
     return (adj_pos, final_momentum_adjoint)
 
 
-def solution(mesh):
+def plain(mesh):
     placed = (
         P(None, None, "brick"),
         P("brick", None),
@@ -144,9 +147,528 @@
         P("kvec", None),
     )
     return jax.shard_map(
-        local,
+        plain_local,
         mesh=mesh,
         in_specs=placed,
         out_specs=(P(None, "brick"), P(None, "brick")),
         check_vma=False,
     )
+
+
+MESH = pl.DeviceIdType.MESH
+GROUP = 8
+MOM = 10
+LANES = 128
+F32, BF16 = jnp.float32, jnp.bfloat16
+two_over_pi = 2.0 / math.pi
+half_pi_parts = (1.5703125, 4.837512969970703125e-4, 7.549789948768648e-8)
+
+
+def sin_cos(phase):
+    n = jnp.round(phase * two_over_pi)
+    r = phase - n * half_pi_parts[0]
+    r = r - n * half_pi_parts[1]
+    r = r - n * half_pi_parts[2]
+    q = n.astype(jnp.int32)
+    z = r * r
+    s = r + r * z * (-1.6666654611e-1 + z * (8.3321608736e-3 + z * -1.9515295891e-4))
+    c = 1.0 - 0.5 * z + z * z * (
+        4.166664568298827e-2 + z * (-1.388731625493765e-3 + z * 2.443315711809948e-5)
+    )
+    odd = (q & 1) == 1
+    sine = jnp.where(odd, c, s)
+    cosine = jnp.where(odd, s, c)
+    sine = jnp.where((q & 2) == 2, -sine, sine)
+    cosine = jnp.where(((q + 1) & 2) == 2, -cosine, cosine)
+    return sine, cosine
+
+
+def split(x):
+    high = x.astype(BF16)
+    return high, (x - high.astype(F32)).astype(BF16)
+
+
+def wide(x, copies):
+    return jnp.concatenate([x] * copies, axis=1)
+
+
+def fold(x):
+    out = x[0:8]
+    for row in range(8, x.shape[0], 8):
+        out = out + x[row : row + 8]
+    return out
+
+
+def spread(x):
+    for shift in (8, 16, 32, 64):
+        x = x + pltpu.roll(x, shift, 1)
+    return x
+
+
+def kernel(
+    kvecs,
+    prefactor,
+    pos_ref,
+    mom_ref,
+    adj_ref,
+    fma_ref,
+    spec_ref,
+    mass_ref,
+    kint_ref,
+    out_adj,
+    out_fma,
+    pack,
+    landed,
+    flown,
+    rows,
+    sent,
+    qall,
+    kmap,
+    amap,
+    w1,
+    w2,
+    trig,
+    high,
+    low,
+    sums,
+    proj,
+    acc,
+    part,
+    bricks,
+    total,
+    zs,
+    fresh,
+    dirs,
+    send_sem,
+    recv_sem,
+    zsend_sem,
+    zrecv_sem,
+):
+    me = lax.axis_index("brick")
+    mev = lax.axis_index("kvec")
+    atoms = LANES * GROUP
+    kdev = kint_ref.shape[0]
+    steps = pos_ref.shape[0]
+
+    def ahead(off):
+        return lax.rem(me + off, GROUP)
+
+    def behind(off):
+        return lax.rem(me + GROUP - off, GROUP)
+
+    def brick_copy(phase, off, src, dst, target):
+        return pltpu.make_async_remote_copy(
+            src_ref=src,
+            dst_ref=dst,
+            send_sem=send_sem.at[phase, off],
+            recv_sem=recv_sem.at[phase, off],
+            device_id=(target, mev),
+            device_id_type=MESH,
+        )
+
+    barrier = pltpu.get_barrier_semaphore()
+    for off in range(1, GROUP):
+        pl.semaphore_signal(barrier, inc=1, device_id=(ahead(off), mev), device_id_type=MESH)
+    for off in range(1, kvecs):
+        pl.semaphore_signal(
+            barrier, inc=1, device_id=(me, lax.rem(mev + off, kvecs)), device_id_type=MESH
+        )
+
+    species = spec_ref[...]
+    mass = jnp.zeros(species.shape, F32)
+    for kind in range(mass_ref.shape[0]):
+        mass = jnp.where(species == kind, mass_ref[kind], mass)
+    inv_mass = 1.0 / mass
+    pack[...] = jnp.zeros_like(pack)
+    for step in range(steps):
+        pack[3 * step : 3 * step + 3, :] = pos_ref[step]
+    pack[3 * steps : 3 * steps + 3, :] = fma_ref[...] * inv_mass
+    for piece in range(mom_ref.shape[1] // LANES):
+        turned = mom_ref[:, piece * LANES : (piece + 1) * LANES].T
+        sent[2 * piece : 2 * piece + 2] = turned.reshape(2, GROUP, 8, LANES)
+
+    pl.semaphore_wait(barrier, GROUP - 1 + kvecs - 1)
+    copies = []
+    for off in range(1, GROUP):
+        copies.append(
+            brick_copy(0, off, pack, landed.at[off], ahead(off))
+        )
+        copies[-1].start()
+    for off in range(1, GROUP):
+        copies.append(
+            brick_copy(
+                1,
+                off,
+                sent.at[:, ahead(off)],
+                qall.at[off],
+                ahead(off),
+            )
+        )
+        copies[-1].start()
+    rows[:, 0:LANES] = pack[...]
+
+    wave = kint_ref[...].astype(F32) * wavevector_scale
+    kx = jnp.broadcast_to(wave[:, 0:1], (kdev, LANES))
+    ky = jnp.broadcast_to(wave[:, 1:2], (kdev, LANES))
+    kz = jnp.broadcast_to(wave[:, 2:3], (kdev, LANES))
+    ksq = kx * kx + ky * ky + kz * kz
+    weight = jnp.exp(-ksq / 4.0) / jnp.maximum(ksq, 1.0) * prefactor
+    for axis, k in enumerate((kx, ky, kz)):
+        kmap[axis] = k
+        kmap[3 + axis] = weight * k
+    lane = lax.broadcasted_iota(jnp.int32, (1, LANES), 1)
+    used = MOM * 8
+
+    def maps(component):
+        def among(*names):
+            out = component == names[0]
+            for name in names[1:]:
+                out = out | (component == name)
+            return out
+
+        one, none = jnp.ones((1, LANES), F32), jnp.zeros((1, LANES), F32)
+        scale_a = jnp.where(component == 0, one, none)
+        scale_a = jnp.where(among(4, 5, 6), -0.5 * one, scale_a)
+        scale_a = jnp.where(among(7, 8, 9), -one, scale_a)
+        scale_b = jnp.where(among(1, 2, 3), one, none)
+        first = jnp.where(
+            among(1, 4, 7, 8), kx, jnp.where(among(2, 5, 9), ky, jnp.where(among(3, 6), kz, one))
+        )
+        second = jnp.where(
+            among(4), kx, jnp.where(among(5, 7), ky, jnp.where(among(6, 8, 9), kz, one))
+        )
+        return first * second * scale_a, first * scale_b
+
+    room = (LANES - used) // 8
+    amap[0], amap[1] = maps(jnp.where(lane < used, lane // 8, (lane - used) // 8))
+    amap[2], amap[3] = maps(
+        jnp.where(
+            lane < used,
+            lane // 8,
+            jnp.where(lane < used + (MOM - room) * 8, room + (lane - used) // 8, MOM),
+        )
+    )
+
+    for off in range(1, GROUP):
+        copies[off - 1].wait_recv()
+        rows[:, off * LANES : (off + 1) * LANES] = landed[off]
+
+    tile = 16
+
+    def make_trig(step, first, last):
+        @pl.loop(first, last)
+        def _(chunk):
+            at = pl.multiple_of(chunk * tile, tile)
+            phase = 0.0
+            for axis in range(3):
+                phase += wide(kmap[axis, pl.ds(at, tile)], GROUP) * rows[3 * step + axis, :][None]
+            sine, cosine = sin_cos(phase)
+            trig[step, 0, pl.ds(at, tile)] = cosine
+            trig[step, 1, pl.ds(at, tile)] = sine
+            high[step, 0, pl.ds(at, tile)], low[step, 0, pl.ds(at, tile)] = split(cosine)
+            high[step, 1, pl.ds(at, tile)], low[step, 1, pl.ds(at, tile)] = split(sine)
+
+    def along(at, rows_here, direction):
+        out = 0.0
+        for axis in range(3):
+            out += wide(kmap[axis, pl.ds(at, rows_here)], GROUP) * direction(axis)
+        return out
+
+    def make_tangent(step, direction):
+        @pl.loop(0, kdev // tile)
+        def _(chunk):
+            at = pl.multiple_of(chunk * tile, tile)
+            k_dot_dir = along(at, tile, direction)
+            for which in range(2):
+                moved = k_dot_dir * trig[step, which, pl.ds(at, tile)]
+                high[steps, which, pl.ds(at, tile)], low[steps, which, pl.ds(at, tile)] = split(
+                    moved
+                )
+
+    block = 128
+
+    def make_sums(source, slot):
+        @pl.loop(0, kdev // block)
+        def _(chunk):
+            at = pl.multiple_of(chunk * block, block)
+            both = []
+            for which in range(2):
+                wide_sum = jnp.dot(
+                    high[source, which, pl.ds(at, block)], w1[...], preferred_element_type=F32
+                )
+                rest = jnp.dot(
+                    low[source, which, pl.ds(at, block)],
+                    w1[:, 0:LANES],
+                    preferred_element_type=F32,
+                )
+                both.append(wide_sum[:, 0:LANES] + wide_sum[:, LANES:] + rest)
+            a, b = amap[0, pl.ds(at, block)], amap[1, pl.ds(at, block)]
+            sums[slot, 0, pl.ds(at, block)] = spread(a * both[0] - b * both[1])
+            sums[slot, 1, pl.ds(at, block)] = spread(a * both[1] + b * both[0])
+
+    def project(real, imag, at):
+        one = real * amap[0, pl.ds(at, block)] + imag * amap[1, pl.ds(at, block)]
+        two = real * amap[2, pl.ds(at, block)] + imag * amap[3, pl.ds(at, block)]
+        top = one.astype(BF16)
+        rest = jnp.where(lane < used, one - top.astype(F32), two).astype(BF16)
+        return jnp.dot(jnp.concatenate([top, rest], axis=1), w2[...], preferred_element_type=F32)
+
+    def factor_part(step, slot):
+        acc[3:9] = jnp.zeros((6, 8, atoms), F32)
+
+        @pl.loop(0, kdev // block)
+        def _(chunk):
+            at = pl.multiple_of(chunk * block, block)
+            real, imag = sums[slot, 0, pl.ds(at, block)], sums[slot, 1, pl.ds(at, block)]
+            proj[0] = project(real, imag, at)
+            proj[1] = project(imag, -real, at)
+
+            @pl.loop(0, block // tile)
+            def _(inner):
+                here = pl.multiple_of(inner * tile, tile)
+                there = pl.multiple_of(at + here, tile)
+                value = (
+                    trig[step, 0, pl.ds(there, tile)] * proj[0, pl.ds(here, tile)]
+                    + trig[step, 1, pl.ds(there, tile)] * proj[1, pl.ds(here, tile)]
+                )
+                row = 3
+                for axis in range(3):
+                    weighted = wide(kmap[3 + axis, pl.ds(there, tile)], GROUP) * value
+                    for other in range(axis, 3):
+                        acc[row] += fold(wide(kmap[other, pl.ds(there, tile)], GROUP) * weighted)
+                        row += 1
+
+    def tangent_part(step, slot):
+        acc[0:3] = jnp.zeros((3, 8, atoms), F32)
+
+        @pl.loop(0, kdev // block)
+        def _(chunk):
+            at = pl.multiple_of(chunk * block, block)
+            real, imag = sums[slot, 0, pl.ds(at, block)], sums[slot, 1, pl.ds(at, block)]
+            proj[0] = project(real, imag, at)
+            proj[1] = project(-imag, real, at)
+
+            @pl.loop(0, block // tile)
+            def _(inner):
+                here = pl.multiple_of(inner * tile, tile)
+                there = pl.multiple_of(at + here, tile)
+                value = (
+                    trig[step, 0, pl.ds(there, tile)] * proj[0, pl.ds(here, tile)]
+                    - trig[step, 1, pl.ds(there, tile)] * proj[1, pl.ds(here, tile)]
+                )
+                for axis in range(3):
+                    acc[axis] += fold(wide(kmap[3 + axis, pl.ds(there, tile)], GROUP) * value)
+
+    def send_force(step, direction):
+        summed = [jnp.sum(acc[row], axis=0, keepdims=True) for row in range(9)]
+        second = {}
+        row = 3
+        for axis in range(3):
+            for other in range(axis, 3):
+                second[axis, other] = second[other, axis] = summed[row]
+                row += 1
+        part[step] = jnp.zeros((GROUP, 8, LANES), F32)
+        for axis in range(3):
+            out = summed[axis]
+            for other in range(3):
+                out = out - second[axis, other] * direction(other)
+            for off in range(GROUP):
+                part[step, off, axis : axis + 1, :] = out[:, off * LANES : (off + 1) * LANES]
+        started = []
+        for off in range(1, GROUP):
+            started.append(
+                brick_copy(
+                    2 + step,
+                    off,
+                    part.at[step, off],
+                    bricks.at[step, off],
+                    behind(off),
+                )
+            )
+            started[-1].start()
+        return started
+
+    def exchange_force(step, started):
+        for copy in started:
+            copy.wait_recv()
+        out = part[step, 0]
+        for off in range(1, GROUP):
+            out = out + bricks[step, off]
+        total[step] = out
+        zs[step, 0] = out
+        over = []
+        for off in range(1, kvecs):
+            over.append(
+                pltpu.make_async_remote_copy(
+                    src_ref=total.at[step],
+                    dst_ref=zs.at[step, off],
+                    send_sem=zsend_sem.at[step, off],
+                    recv_sem=zrecv_sem.at[step, off],
+                    device_id=(me, lax.rem(mev + off, kvecs)),
+                    device_id_type=MESH,
+                )
+            )
+            over[-1].start()
+        return over
+
+    def finish_force(step, over):
+        for copy in over:
+            copy.wait_recv()
+        out = jnp.zeros((8, LANES), F32)
+        for owner in range(kvecs):
+            off = lax.rem(mev + kvecs - owner, kvecs)
+            share = zs[step, 0]
+            for other in range(1, kvecs):
+                share = jnp.where(off == other, zs[step, other], share)
+            out = out + share
+        return out[0:3]
+
+    def first_direction(axis):
+        return rows[3 * steps + axis, :][None]
+
+    last = steps - 1
+    chunks = kdev // tile
+    make_trig(last, 0, chunks)
+    make_tangent(last, first_direction)
+    for off in range(1, GROUP):
+        copies[GROUP - 1 + off - 1].wait_recv()
+    moments = jnp.concatenate(
+        [sent[:, pl.ds(me, 1)].reshape(used, LANES)]
+        + [qall[off].reshape(used, LANES) for off in range(1, GROUP)],
+        axis=1,
+    )
+    q_high, q_low = split(moments)
+    turned = jnp.concatenate([moments, jnp.zeros((LANES - used, atoms), F32)], axis=0).T
+    w1[:, 0:LANES], w1[:, LANES:] = split(turned)
+    fits = LANES - used
+    w2[0:used] = q_high
+    w2[used:LANES] = q_low[0:fits]
+    w2[LANES : LANES + used] = q_high
+    w2[LANES + used : LANES + 2 * used - fits] = q_low[fits:]
+    w2[LANES + 2 * used - fits :] = jnp.zeros((2 * LANES - (LANES + 2 * used - fits), atoms), BF16)
+
+    adj, fma = adj_ref[...], fma_ref[...]
+    direction = first_direction
+    for step in reversed(range(steps)):
+        if step == last:
+            make_sums(step, 0)
+            factor_part(step, 0)
+        make_sums(steps, 1)
+        tangent_part(step, 1)
+        started = send_force(step, direction)
+        if step > 0:
+            make_trig(step - 1, 0, chunks // 2)
+        over = exchange_force(step, started)
+        if step > 0:
+            make_trig(step - 1, chunks // 2, chunks)
+        force = finish_force(step, over)
+        adj = adj - time_step * force
+        fma = fma + time_step * adj
+        copies += started + over
+        if step > 0:
+            fresh[step - 1] = jnp.concatenate([fma * inv_mass, jnp.zeros((5, LANES), F32)], axis=0)
+            sends = []
+            for off in range(1, GROUP):
+                sends.append(
+                    brick_copy(
+                        2 + steps + step - 1,
+                        off,
+                        fresh.at[step - 1],
+                        flown.at[step - 1, off],
+                        ahead(off),
+                    )
+                )
+                sends[-1].start()
+            dirs[step - 1, :, 0:LANES] = fresh[step - 1]
+            make_sums(step - 1, 0)
+            factor_part(step - 1, 0)
+            for off in range(1, GROUP):
+                sends[off - 1].wait_recv()
+                dirs[step - 1, :, off * LANES : (off + 1) * LANES] = flown[step - 1, off]
+            copies += sends
+
+            def direction(axis, step=step):
+                return dirs[step - 1, axis, :][None]
+
+            make_tangent(step - 1, direction)
+    out_adj[...] = adj
+    out_fma[...] = fma
+    for copy in copies:
+        copy.wait_send()
+
+
+def fused(kvecs, bricks, positions, moments, adj_pos, final_momentum_adjoint, species, masses, kint):
+    steps, _, here = positions.shape
+    kdev = kint.shape[0]
+    atoms = here * GROUP
+    phases = 2 + 2 * steps - 1
+    prefactor = energy_scale / math.sqrt(here * bricks)
+    vmem = pl.BlockSpec(memory_space=pltpu.VMEM)
+    small = jax.ShapeDtypeStruct((3, here), F32)
+    return pl.pallas_call(
+        functools.partial(kernel, kvecs, prefactor),
+        out_shape=(small, small),
+        in_specs=[vmem] * 5 + [pl.BlockSpec(memory_space=pltpu.SMEM), vmem],
+        out_specs=(vmem, vmem),
+        scratch_shapes=[
+            pltpu.VMEM((16, here), F32),
+            pltpu.VMEM((GROUP, 16, here), F32),
+            pltpu.VMEM((steps, GROUP, 8, here), F32),
+            pltpu.VMEM((16, atoms), F32),
+            pltpu.VMEM((MOM, GROUP, 8, here), F32),
+            pltpu.VMEM((GROUP, MOM, 8, here), F32),
+            pltpu.VMEM((6, kdev, LANES), F32),
+            pltpu.VMEM((4, kdev, LANES), F32),
+            pltpu.VMEM((atoms, 2 * LANES), BF16),
+            pltpu.VMEM((2 * LANES, atoms), BF16),
+            pltpu.VMEM((steps, 2, kdev, atoms), F32),
+            pltpu.VMEM((steps + 1, 2, kdev, atoms), BF16),
+            pltpu.VMEM((steps + 1, 2, kdev, atoms), BF16),
+            pltpu.VMEM((2, 2, kdev, LANES), F32),
+            pltpu.VMEM((2, 128, atoms), F32),
+            pltpu.VMEM((9, 8, atoms), F32),
+            pltpu.VMEM((steps, GROUP, 8, here), F32),
+            pltpu.VMEM((steps, GROUP, 8, here), F32),
+            pltpu.VMEM((steps, 8, here), F32),
+            pltpu.VMEM((steps, kvecs, 8, here), F32),
+            pltpu.VMEM((steps, 8, here), F32),
+            pltpu.VMEM((steps, 8, atoms), F32),
+            pltpu.SemaphoreType.DMA((phases, GROUP)),
+            pltpu.SemaphoreType.DMA((phases, GROUP)),
+            pltpu.SemaphoreType.DMA((steps, kvecs)),
+            pltpu.SemaphoreType.DMA((steps, kvecs)),
+        ],
+        compiler_params=pltpu.CompilerParams(
+            collective_id=0, has_side_effects=True, vmem_limit_bytes=48 << 20
+        ),
+    )(
+        positions,
+        moments,
+        adj_pos,
+        final_momentum_adjoint,
+        species.reshape(1, here),
+        masses,
+        kint,
+    )
+
+
+def solution(mesh):
+    bricks, kvecs = mesh.shape["brick"], mesh.shape["kvec"]
+    if bricks != GROUP:
+        return plain(mesh)
+    placed = (
+        P(None, None, "brick"),
+        P("brick", None),
+        P(None, "brick"),
+        P(None, "brick"),
+        P("brick"),
+        P(),
+        P("kvec", None),
+    )
+    return jax.shard_map(
+        functools.partial(fused, kvecs, bricks),
+        mesh=mesh,
+        in_specs=placed,
+        out_specs=(P(None, "brick"), P(None, "brick")),
+        check_vma=False,
+    )

time: 209 us -> 50.6 us (0.24)
  waiting for transfers between devices: 107 us -> 0 us
  Pallas kernels: 0 us -> 46.2 us
  matrix products: 26.8 us -> 0 us
  blocking collectives: 23.5 us -> 0 us
  other arithmetic: 19.6 us -> 0 us
  between operations: 14.3 us -> 0.67 us
  local copies, waits for them, and re-layouts: 16.8 us -> 3.51 us
    psum x2 -> x0, waiting for transfers between devices: 107 us -> none  [local(): lax.psum((fac_re, fac_im, -tan_im, tangent_real_part), 'brick')]
    pallas_call x0 -> x1, Pallas kernels: none -> 46.2 us  [fused(): pl.pallas_call(functools.partial(kernel, kvecs, prefactor), out_shape=(sm...]
    dot_general x17 -> x0, matrix products: 26.8 us -> none  [the longest x2 10.1 us: tangent_force(): projected = jnp.einsum('jkf,af->jka', stacked, moments, precision=exact)]
    psum x2 -> x0, blocking collectives: 23.5 us -> none  [local(): force = lax.psum(partial_force, 'kvec')]
    add x8 -> x0, local copies, waits for them, and re-layouts: 12.8 us -> none  [weave_terms(): leading_dimension[:, None, :] * acoef[:, :, None]]
    add x5 -> x0, other arithmetic: 6.95 us -> none  [the longest x2 5.07 us: weave_terms(): leading_dimension[:, None, :] * acoef[:, :, None]]
    neg x6 -> x0, other arithmetic: 4.87 us -> none  [the longest x2 1.8 us: tangent_force(): -factor_re]
    dot_general x2 -> x0, other arithmetic: 3.85 us -> none  [the longest x1 3.56 us: moment_sums(): jnp.einsum('km,kmc->kc', acoef, sine_component, precision=exact)]
  transfers between devices with their start and end apart: 2 -> 0, of which waited for: 2 -> 0; matrix products, arithmetic and copies ran while one was open for 1% -> 0% of each run, Pallas kernels for 0% -> 0%
where the time goes in v1:
time: 50.6 us; the launch traced here: 50.3 us
  Pallas kernels  46.2 us (91%)
  local copies, waits for them, and re-layouts  3.51 us (7%)
  between operations  0.67 us (1%)
    pallas_call x1, Pallas kernels, fused(): pl.pallas_call(functools.partial(kernel, kvecs, prefactor), out_shape=(sm...  46.2 us
    unnamed x16, local copies, waits for them, and re-layouts  3.51 us

profile of v1, /device:TPU:0, one launch (start us, length us, event | category | flops | bytes accessed | tf_op | source)
XLA Modules:
  0.0 50.3 jit_solution(12582984678916030430)
XLA Ops:
  0.6 0.0 copy-start.5
  0.6 0.7 %copy.9.pos_ref = f32[2,3,128]{2,1,0:T(4,128)S(1)} copy(f32[2,3,128]{2,0,1:T(2,128)} %param.7) | data formatting | bytes 6144 | tf_op args[0]
  1.3 0.0 copy-done.5
  1.3 0.0 copy-start.1
  1.3 0.0 copy-start.2
  1.3 0.0 copy-start.3
  1.3 0.0 copy-start.4
  1.4 0.1 copy.10.kint_ref
  1.5 0.5 %copy-done.1 = f32[3,128]{1,0:T(4,128)S(1)} copy-done((f32[3,128]{1,0:T(4,128)S(1)}, f32[3,128]{1,0:T(4,128)}, u32[]{:S(2)}) %copy-start.1) | copy-done | bytes 1560
  2.0 0.0 copy-done.2
  2.0 0.0 copy-done.3
  2.0 0.0 copy-done.4
  2.0 0.0 copy-start
  2.0 1.0 %copy-done = f32[128,640]{1,0:T(8,128)S(1)} copy-done((f32[128,640]{1,0:T(8,128)S(1)}, f32[128,640]{1,0:T(8,128)}, u32[]{:S(2)}) %copy-start) | copy-done | bytes 327704
  3.0 46.2 %shard_map.86 = (f32[3,128]{1,0:T(4,128)S(1)}, f32[3,128]{1,0:T(4,128)S(1)}) custom-call(f32[2,3,128]{2,1,0:T(4,128)S(1)} %copy.9.pos_ref, f32[128,640]{1,0:T(8,128)S(1)} %copy-done, f32[3,128]{1,0:T(4,128)S(1)} %copy-done.1, f32[3,128]{1,0:T(4,128)S(1)} %copy-done.2, s32[1,128]{1,0:T(1,128)S(1)} %bitcast.1, f32[6]{0:T(128)S(1)} %copy-done.4, ...), custom_call_target="tpu_custom_call" | custom-call | tf_op jit(solution)/shard_map/pallas_call | solution.py:608
  49.2 0.6 %copy.13 = f32[3,128]{1,0:T(4,128)} copy(f32[3,128]{1,0:T(4,128)S(1)} %get-tuple-element.4) | data formatting | bytes 3072
  49.8 0.6 %copy.14 = f32[3,128]{1,0:T(4,128)} copy(f32[3,128]{1,0:T(4,128)S(1)} %get-tuple-element.5) | data formatting | bytes 3072
Async XLA Ops:
  0.6 0.7 %copy-start.5 = (s32[384,3]{0,1:T(4,128)S(1)}, s32[384,3]{0,1:T(4,128)}, u32[]{:S(2)}) copy-start(s32[384,3]{0,1:T(4,128)} %param.13) | copy-start | bytes 13828
  1.3 0.7 %copy-start.1 = (f32[3,128]{1,0:T(4,128)S(1)}, f32[3,128]{1,0:T(4,128)}, u32[]{:S(2)}) copy-start(f32[3,128]{1,0:T(4,128)} %adj_ref.1) | copy-start | bytes 4612
  1.3 0.7 %copy-start.2 = (f32[3,128]{1,0:T(4,128)S(1)}, f32[3,128]{1,0:T(4,128)}, u32[]{:S(2)}) copy-start(f32[3,128]{1,0:T(4,128)} %fma_ref.1) | copy-start | bytes 4612
  1.3 0.7 %copy-start.3 = (s32[128]{0:T(128)S(1)}, s32[128]{0:T(128)}, u32[]{:S(2)}) copy-start(s32[128]{0:T(128)} %param.11) | copy-start | bytes 1540
  1.3 0.7 %copy-start.4 = (f32[6]{0:T(128)S(1)}, f32[6]{0:T(128)}, u32[]{:S(2)}) copy-start(f32[6]{0:T(128)} %mass_ref.1) | copy-start | bytes 76
  2.0 1.0 %copy-start = (f32[128,640]{1,0:T(8,128)S(1)}, f32[128,640]{1,0:T(8,128)}, u32[]{:S(2)}) copy-start(f32[128,640]{1,0:T(8,128)} %mom_ref.1) | copy-start | bytes 983044

commit v2 on v1

--- a/solution.py
+++ b/solution.py
@@ -235,8 +235,6 @@
     acc,
     part,
     bricks,
-    total,
-    zs,
     fresh,
     dirs,
     send_sem,
@@ -267,12 +265,15 @@
         )
 
     barrier = pltpu.get_barrier_semaphore()
-    for off in range(1, GROUP):
-        pl.semaphore_signal(barrier, inc=1, device_id=(ahead(off), mev), device_id_type=MESH)
-    for off in range(1, kvecs):
-        pl.semaphore_signal(
-            barrier, inc=1, device_id=(me, lax.rem(mev + off, kvecs)), device_id_type=MESH
-        )
+    for over in range(kvecs):
+        for off in range(GROUP):
+            if over > 0 or off > 0:
+                pl.semaphore_signal(
+                    barrier,
+                    inc=1,
+                    device_id=(ahead(off), lax.rem(mev + over, kvecs)),
+                    device_id_type=MESH,
+                )
 
     species = spec_ref[...]
     mass = jnp.zeros(species.shape, F32)
@@ -287,7 +288,7 @@
         turned = mom_ref[:, piece * LANES : (piece + 1) * LANES].T
         sent[2 * piece : 2 * piece + 2] = turned.reshape(2, GROUP, 8, LANES)
 
-    pl.semaphore_wait(barrier, GROUP - 1 + kvecs - 1)
+    pl.semaphore_wait(barrier, GROUP * kvecs - 1)
     copies = []
     for off in range(1, GROUP):
         copies.append(
@@ -385,79 +386,67 @@
                     moved
                 )
 
-    block = 128
-
-    def make_sums(source, slot):
-        @pl.loop(0, kdev // block)
-        def _(chunk):
-            at = pl.multiple_of(chunk * block, block)
-            both = []
-            for which in range(2):
-                wide_sum = jnp.dot(
-                    high[source, which, pl.ds(at, block)], w1[...], preferred_element_type=F32
-                )
-                rest = jnp.dot(
-                    low[source, which, pl.ds(at, block)],
-                    w1[:, 0:LANES],
-                    preferred_element_type=F32,
-                )
-                both.append(wide_sum[:, 0:LANES] + wide_sum[:, LANES:] + rest)
-            a, b = amap[0, pl.ds(at, block)], amap[1, pl.ds(at, block)]
-            sums[slot, 0, pl.ds(at, block)] = spread(a * both[0] - b * both[1])
-            sums[slot, 1, pl.ds(at, block)] = spread(a * both[1] + b * both[0])
-
-    def project(real, imag, at):
-        one = real * amap[0, pl.ds(at, block)] + imag * amap[1, pl.ds(at, block)]
-        two = real * amap[2, pl.ds(at, block)] + imag * amap[3, pl.ds(at, block)]
+    def make_sums(source, slots):
+        count = 2 * len(slots) * kdev
+        here = pl.ds(source, len(slots))
+        wide_sum = jnp.dot(
+            high[here].reshape(count, atoms), w1[...], preferred_element_type=F32
+        )
+        rest = jnp.dot(
+            low[here].reshape(count, atoms), w1[:, 0:LANES], preferred_element_type=F32
+        )
+        both = wide_sum[:, 0:LANES] + wide_sum[:, LANES:] + rest
+        a, b = amap[0], amap[1]
+        for place, slot in enumerate(slots):
+            cos_sum = both[2 * place * kdev : (2 * place + 1) * kdev]
+            sin_sum = both[(2 * place + 1) * kdev : (2 * place + 2) * kdev]
+            sums[slot, 0] = spread(a * cos_sum - b * sin_sum)
+            sums[slot, 1] = spread(a * sin_sum + b * cos_sum)
+
+    def operand(real, imag):
+        one = real * amap[0] + imag * amap[1]
+        two = real * amap[2] + imag * amap[3]
         top = one.astype(BF16)
         rest = jnp.where(lane < used, one - top.astype(F32), two).astype(BF16)
-        return jnp.dot(jnp.concatenate([top, rest], axis=1), w2[...], preferred_element_type=F32)
+        return jnp.concatenate([top, rest], axis=1)
+
+    def project(first, second):
+        both = jnp.concatenate([operand(*first), operand(*second)], axis=0)
+        proj[...] = jnp.dot(both, w2[...], preferred_element_type=F32)
 
     def factor_part(step, slot):
         acc[3:9] = jnp.zeros((6, 8, atoms), F32)
-
-        @pl.loop(0, kdev // block)
+        real, imag = sums[slot, 0], sums[slot, 1]
+        project((real, imag), (imag, -real))
+
+        @pl.loop(0, kdev // tile)
         def _(chunk):
-            at = pl.multiple_of(chunk * block, block)
-            real, imag = sums[slot, 0, pl.ds(at, block)], sums[slot, 1, pl.ds(at, block)]
-            proj[0] = project(real, imag, at)
-            proj[1] = project(imag, -real, at)
-
-            @pl.loop(0, block // tile)
-            def _(inner):
-                here = pl.multiple_of(inner * tile, tile)
-                there = pl.multiple_of(at + here, tile)
-                value = (
-                    trig[step, 0, pl.ds(there, tile)] * proj[0, pl.ds(here, tile)]
-                    + trig[step, 1, pl.ds(there, tile)] * proj[1, pl.ds(here, tile)]
-                )
-                row = 3
-                for axis in range(3):
-                    weighted = wide(kmap[3 + axis, pl.ds(there, tile)], GROUP) * value
-                    for other in range(axis, 3):
-                        acc[row] += fold(wide(kmap[other, pl.ds(there, tile)], GROUP) * weighted)
-                        row += 1
+            at = pl.multiple_of(chunk * tile, tile)
+            value = (
+                trig[step, 0, pl.ds(at, tile)] * proj[pl.ds(at, tile)]
+                + trig[step, 1, pl.ds(at, tile)] * proj[pl.ds(pl.multiple_of(kdev + at, tile), tile)]
+            )
+            row = 3
+            for axis in range(3):
+                weighted = wide(kmap[3 + axis, pl.ds(at, tile)], GROUP) * value
+                for other in range(axis, 3):
+                    acc[row] += fold(wide(kmap[other, pl.ds(at, tile)], GROUP) * weighted)
+                    row += 1
 
     def tangent_part(step, slot):
         acc[0:3] = jnp.zeros((3, 8, atoms), F32)
-
-        @pl.loop(0, kdev // block)
+        real, imag = sums[slot, 0], sums[slot, 1]
+        project((real, imag), (-imag, real))
+
+        @pl.loop(0, kdev // tile)
         def _(chunk):
-            at = pl.multiple_of(chunk * block, block)
-            real, imag = sums[slot, 0, pl.ds(at, block)], sums[slot, 1, pl.ds(at, block)]
-            proj[0] = project(real, imag, at)
-            proj[1] = project(-imag, real, at)
-
-            @pl.loop(0, block // tile)
-            def _(inner):
-                here = pl.multiple_of(inner * tile, tile)
-                there = pl.multiple_of(at + here, tile)
-                value = (
-                    trig[step, 0, pl.ds(there, tile)] * proj[0, pl.ds(here, tile)]
-                    - trig[step, 1, pl.ds(there, tile)] * proj[1, pl.ds(here, tile)]
-                )
-                for axis in range(3):
-                    acc[axis] += fold(wide(kmap[3 + axis, pl.ds(there, tile)], GROUP) * value)
+            at = pl.multiple_of(chunk * tile, tile)
+            value = (
+                trig[step, 0, pl.ds(at, tile)] * proj[pl.ds(at, tile)]
+                - trig[step, 1, pl.ds(at, tile)] * proj[pl.ds(pl.multiple_of(kdev + at, tile), tile)]
+            )
+            for axis in range(3):
+                acc[axis] += fold(wide(kmap[3 + axis, pl.ds(at, tile)], GROUP) * value)
 
     def send_force(step, direction):
         summed = [jnp.sum(acc[row], axis=0, keepdims=True) for row in range(9)]
@@ -475,51 +464,38 @@
             for off in range(GROUP):
                 part[step, off, axis : axis + 1, :] = out[:, off * LANES : (off + 1) * LANES]
         started = []
-        for off in range(1, GROUP):
-            started.append(
-                brick_copy(
-                    2 + step,
-                    off,
-                    part.at[step, off],
-                    bricks.at[step, off],
-                    behind(off),
+        for over in range(kvecs):
+            for off in range(GROUP):
+                if over == 0 and off == 0:
+                    continue
+                started.append(
+                    pltpu.make_async_remote_copy(
+                        src_ref=part.at[step, off],
+                        dst_ref=bricks.at[step, over, off],
+                        send_sem=zsend_sem.at[step, over, off],
+                        recv_sem=zrecv_sem.at[step, over, off],
+                        device_id=(behind(off), lax.rem(mev + over, kvecs)),
+                        device_id_type=MESH,
+                    )
                 )
-            )
-            started[-1].start()
+                started[-1].start()
         return started
 
-    def exchange_force(step, started):
+    def finish_force(step, started):
         for copy in started:
             copy.wait_recv()
-        out = part[step, 0]
-        for off in range(1, GROUP):
-            out = out + bricks[step, off]
-        total[step] = out
-        zs[step, 0] = out
-        over = []
-        for off in range(1, kvecs):
-            over.append(
-                pltpu.make_async_remote_copy(
-                    src_ref=total.at[step],
-                    dst_ref=zs.at[step, off],
-                    send_sem=zsend_sem.at[step, off],
-                    recv_sem=zrecv_sem.at[step, off],
-                    device_id=(me, lax.rem(mev + off, kvecs)),
-                    device_id_type=MESH,
-                )
-            )
-            over[-1].start()
-        return over
-
-    def finish_force(step, over):
-        for copy in over:
-            copy.wait_recv()
+        shares = []
+        for over in range(kvecs):
+            out = part[step, 0] if over == 0 else bricks[step, over, 0]
+            for off in range(1, GROUP):
+                out = out + bricks[step, over, off]
+            shares.append(out)
         out = jnp.zeros((8, LANES), F32)
         for owner in range(kvecs):
-            off = lax.rem(mev + kvecs - owner, kvecs)
-            share = zs[step, 0]
+            over = lax.rem(mev + kvecs - owner, kvecs)
+            share = shares[0]
             for other in range(1, kvecs):
-                share = jnp.where(off == other, zs[step, other], share)
+                share = jnp.where(over == other, shares[other], share)
             out = out + share
         return out[0:3]
 
@@ -551,20 +527,18 @@
     direction = first_direction
     for step in reversed(range(steps)):
         if step == last:
-            make_sums(step, 0)
+            make_sums(step, (0, 1))
             factor_part(step, 0)
-        make_sums(steps, 1)
+        else:
+            make_sums(steps, (1,))
         tangent_part(step, 1)
         started = send_force(step, direction)
         if step > 0:
-            make_trig(step - 1, 0, chunks // 2)
-        over = exchange_force(step, started)
-        if step > 0:
-            make_trig(step - 1, chunks // 2, chunks)
-        force = finish_force(step, over)
+            make_trig(step - 1, 0, chunks)
+        force = finish_force(step, started)
         adj = adj - time_step * force
         fma = fma + time_step * adj
-        copies += started + over
+        copies += started
         if step > 0:
             fresh[step - 1] = jnp.concatenate([fma * inv_mass, jnp.zeros((5, LANES), F32)], axis=0)
             sends = []
@@ -580,7 +554,7 @@
                 )
                 sends[-1].start()
             dirs[step - 1, :, 0:LANES] = fresh[step - 1]
-            make_sums(step - 1, 0)
+            make_sums(step - 1, (0,))
             factor_part(step - 1, 0)
             for off in range(1, GROUP):
                 sends[off - 1].wait_recv()
@@ -625,18 +599,16 @@
             pltpu.VMEM((steps + 1, 2, kdev, atoms), BF16),
             pltpu.VMEM((steps + 1, 2, kdev, atoms), BF16),
             pltpu.VMEM((2, 2, kdev, LANES), F32),
-            pltpu.VMEM((2, 128, atoms), F32),
+            pltpu.VMEM((2 * kdev, atoms), F32),
             pltpu.VMEM((9, 8, atoms), F32),
             pltpu.VMEM((steps, GROUP, 8, here), F32),
-            pltpu.VMEM((steps, GROUP, 8, here), F32),
-            pltpu.VMEM((steps, 8, here), F32),
-            pltpu.VMEM((steps, kvecs, 8, here), F32),
+            pltpu.VMEM((steps, kvecs, GROUP, 8, here), F32),
             pltpu.VMEM((steps, 8, here), F32),
             pltpu.VMEM((steps, 8, atoms), F32),
             pltpu.SemaphoreType.DMA((phases, GROUP)),
             pltpu.SemaphoreType.DMA((phases, GROUP)),
-            pltpu.SemaphoreType.DMA((steps, kvecs)),
-            pltpu.SemaphoreType.DMA((steps, kvecs)),
+            pltpu.SemaphoreType.DMA((steps, kvecs, GROUP)),
+            pltpu.SemaphoreType.DMA((steps, kvecs, GROUP)),
         ],
         compiler_params=pltpu.CompilerParams(
             collective_id=0, has_side_effects=True, vmem_limit_bytes=48 << 20

time: 50.6 us -> 44.1 us (0.87)
  Pallas kernels: 46.2 us -> 39.7 us
    pallas_call x1, Pallas kernels: 46.2 us -> 39.7 us  [fused(): pl.pallas_call(functools.partial(kernel, kvecs, prefactor), out_shape=(sm...]
where the time goes in v2:
time: 44.1 us; the launch traced here: 43.9 us
  Pallas kernels  39.7 us (90%)
  local copies, waits for them, and re-layouts  3.51 us (8%)
  between operations  0.67 us (2%)
    pallas_call x1, Pallas kernels, fused(): pl.pallas_call(functools.partial(kernel, kvecs, prefactor), out_shape=(sm...  39.7 us
    unnamed x16, local copies, waits for them, and re-layouts  3.51 us

profile of v2, /device:TPU:0, one launch (start us, length us, event | category | flops | bytes accessed | tf_op | source)
XLA Modules:
  0.0 43.9 jit_solution(7357749747669272528)
XLA Ops:
  0.6 0.0 copy-start.5
  0.6 0.7 %copy.9.pos_ref = f32[2,3,128]{2,1,0:T(4,128)S(1)} copy(f32[2,3,128]{2,0,1:T(2,128)} %param.7) | data formatting | bytes 6144 | tf_op args[0]
  1.3 0.0 copy-done.5
  1.3 0.0 copy-start.1
  1.3 0.0 copy-start.2
  1.3 0.0 copy-start.3
  1.3 0.0 copy-start.4
  1.4 0.1 copy.10.kint_ref
  1.5 0.5 %copy-done.1 = f32[3,128]{1,0:T(4,128)S(1)} copy-done((f32[3,128]{1,0:T(4,128)S(1)}, f32[3,128]{1,0:T(4,128)}, u32[]{:S(2)}) %copy-start.1) | copy-done | bytes 1560
  2.0 0.0 copy-done.2
  2.0 0.0 copy-done.3
  2.0 0.0 copy-done.4
  2.0 0.0 copy-start
  2.0 1.0 %copy-done = f32[128,640]{1,0:T(8,128)S(1)} copy-done((f32[128,640]{1,0:T(8,128)S(1)}, f32[128,640]{1,0:T(8,128)}, u32[]{:S(2)}) %copy-start) | copy-done | bytes 327704
  3.0 39.7 %shard_map.86 = (f32[3,128]{1,0:T(4,128)S(1)}, f32[3,128]{1,0:T(4,128)S(1)}) custom-call(f32[2,3,128]{2,1,0:T(4,128)S(1)} %copy.9.pos_ref, f32[128,640]{1,0:T(8,128)S(1)} %copy-done, f32[3,128]{1,0:T(4,128)S(1)} %copy-done.1, f32[3,128]{1,0:T(4,128)S(1)} %copy-done.2, s32[1,128]{1,0:T(1,128)S(1)} %bitcast.1, f32[6]{0:T(128)S(1)} %copy-done.4, ...), custom_call_target="tpu_custom_call" | custom-call | tf_op jit(solution)/shard_map/pallas_call | solution.py:582
  42.7 0.6 %copy.13 = f32[3,128]{1,0:T(4,128)} copy(f32[3,128]{1,0:T(4,128)S(1)} %get-tuple-element.4) | data formatting | bytes 3072
  43.3 0.6 %copy.14 = f32[3,128]{1,0:T(4,128)} copy(f32[3,128]{1,0:T(4,128)S(1)} %get-tuple-element.5) | data formatting | bytes 3072
Async XLA Ops:
  0.6 0.7 %copy-start.5 = (s32[384,3]{0,1:T(4,128)S(1)}, s32[384,3]{0,1:T(4,128)}, u32[]{:S(2)}) copy-start(s32[384,3]{0,1:T(4,128)} %param.13) | copy-start | bytes 13828
  1.3 0.7 %copy-start.1 = (f32[3,128]{1,0:T(4,128)S(1)}, f32[3,128]{1,0:T(4,128)}, u32[]{:S(2)}) copy-start(f32[3,128]{1,0:T(4,128)} %adj_ref.1) | copy-start | bytes 4612
  1.3 0.7 %copy-start.2 = (f32[3,128]{1,0:T(4,128)S(1)}, f32[3,128]{1,0:T(4,128)}, u32[]{:S(2)}) copy-start(f32[3,128]{1,0:T(4,128)} %fma_ref.1) | copy-start | bytes 4612
  1.3 0.7 %copy-start.3 = (s32[128]{0:T(128)S(1)}, s32[128]{0:T(128)}, u32[]{:S(2)}) copy-start(s32[128]{0:T(128)} %param.11) | copy-start | bytes 1540
  1.3 0.7 %copy-start.4 = (f32[6]{0:T(128)S(1)}, f32[6]{0:T(128)}, u32[]{:S(2)}) copy-start(f32[6]{0:T(128)} %mass_ref.1) | copy-start | bytes 76
  2.0 1.0 %copy-start = (f32[128,640]{1,0:T(8,128)S(1)}, f32[128,640]{1,0:T(8,128)}, u32[]{:S(2)}) copy-start(f32[128,640]{1,0:T(8,128)} %mom_ref.1) | copy-start | bytes 983044

commit v3 on v2

--- a/solution.py
+++ b/solution.py
@@ -209,7 +209,7 @@
     kvecs,
     prefactor,
     pos_ref,
-    mom_ref,
+    mom_hbm,
     adj_ref,
     fma_ref,
     spec_ref,
@@ -217,6 +217,8 @@
     kint_ref,
     out_adj,
     out_fma,
+    mom_ref,
+    mom_sem,
     pack,
     landed,
     flown,
@@ -264,6 +266,8 @@
             device_id_type=MESH,
         )
 
+    fetch = pltpu.make_async_copy(mom_hbm, mom_ref, mom_sem)
+    fetch.start()
     barrier = pltpu.get_barrier_semaphore()
     for over in range(kvecs):
         for off in range(GROUP):
@@ -284,29 +288,10 @@
     for step in range(steps):
         pack[3 * step : 3 * step + 3, :] = pos_ref[step]
     pack[3 * steps : 3 * steps + 3, :] = fma_ref[...] * inv_mass
+    fetch.wait()
     for piece in range(mom_ref.shape[1] // LANES):
         turned = mom_ref[:, piece * LANES : (piece + 1) * LANES].T
         sent[2 * piece : 2 * piece + 2] = turned.reshape(2, GROUP, 8, LANES)
-
-    pl.semaphore_wait(barrier, GROUP * kvecs - 1)
-    copies = []
-    for off in range(1, GROUP):
-        copies.append(
-            brick_copy(0, off, pack, landed.at[off], ahead(off))
-        )
-        copies[-1].start()
-    for off in range(1, GROUP):
-        copies.append(
-            brick_copy(
-                1,
-                off,
-                sent.at[:, ahead(off)],
-                qall.at[off],
-                ahead(off),
-            )
-        )
-        copies[-1].start()
-    rows[:, 0:LANES] = pack[...]
 
     wave = kint_ref[...].astype(F32) * wavevector_scale
     kx = jnp.broadcast_to(wave[:, 0:1], (kdev, LANES))
@@ -349,6 +334,26 @@
             jnp.where(lane < used + (MOM - room) * 8, room + (lane - used) // 8, MOM),
         )
     )
+
+    pl.semaphore_wait(barrier, GROUP * kvecs - 1)
+    copies = []
+    for off in range(1, GROUP):
+        copies.append(
+            brick_copy(0, off, pack, landed.at[off], ahead(off))
+        )
+        copies[-1].start()
+    for off in range(1, GROUP):
+        copies.append(
+            brick_copy(
+                1,
+                off,
+                sent.at[:, ahead(off)],
+                qall.at[off],
+                ahead(off),
+            )
+        )
+        copies[-1].start()
+    rows[:, 0:LANES] = pack[...]
 
     for off in range(1, GROUP):
         copies[off - 1].wait_recv()
@@ -456,7 +461,7 @@
             for other in range(axis, 3):
                 second[axis, other] = second[other, axis] = summed[row]
                 row += 1
-        part[step] = jnp.zeros((GROUP, 8, LANES), F32)
+        part[step] = jnp.zeros((GROUP, 4, LANES), F32)
         for axis in range(3):
             out = summed[axis]
             for other in range(3):
@@ -464,7 +469,7 @@
             for off in range(GROUP):
                 part[step, off, axis : axis + 1, :] = out[:, off * LANES : (off + 1) * LANES]
         started = []
-        for over in range(kvecs):
+        for over in reversed(range(kvecs)):
             for off in range(GROUP):
                 if over == 0 and off == 0:
                     continue
@@ -490,7 +495,7 @@
             for off in range(1, GROUP):
                 out = out + bricks[step, over, off]
             shares.append(out)
-        out = jnp.zeros((8, LANES), F32)
+        out = jnp.zeros((4, LANES), F32)
         for owner in range(kvecs):
             over = lax.rem(mev + kvecs - owner, kvecs)
             share = shares[0]
@@ -582,9 +587,11 @@
     return pl.pallas_call(
         functools.partial(kernel, kvecs, prefactor),
         out_shape=(small, small),
-        in_specs=[vmem] * 5 + [pl.BlockSpec(memory_space=pltpu.SMEM), vmem],
+        in_specs=[vmem, pl.BlockSpec(memory_space=pl.ANY)] + [vmem] * 3 + [pl.BlockSpec(memory_space=pltpu.SMEM), vmem],
         out_specs=(vmem, vmem),
         scratch_shapes=[
+            pltpu.VMEM(moments.shape, F32),
+            pltpu.SemaphoreType.DMA,
             pltpu.VMEM((16, here), F32),
             pltpu.VMEM((GROUP, 16, here), F32),
             pltpu.VMEM((steps, GROUP, 8, here), F32),
@@ -601,8 +608,8 @@
             pltpu.VMEM((2, 2, kdev, LANES), F32),
             pltpu.VMEM((2 * kdev, atoms), F32),
             pltpu.VMEM((9, 8, atoms), F32),
-            pltpu.VMEM((steps, GROUP, 8, here), F32),
-            pltpu.VMEM((steps, kvecs, GROUP, 8, here), F32),
+            pltpu.VMEM((steps, GROUP, 4, here), F32),
+            pltpu.VMEM((steps, kvecs, GROUP, 4, here), F32),
             pltpu.VMEM((steps, 8, here), F32),
             pltpu.VMEM((steps, 8, atoms), F32),
             pltpu.SemaphoreType.DMA((phases, GROUP)),

time: 44.1 us -> 42.7 us (0.968)
  Pallas kernels: 39.7 us -> 38.3 us
    pallas_call x1, Pallas kernels: 39.7 us -> 38.3 us  [fused(): pl.pallas_call(functools.partial(kernel, kvecs, prefactor), out_shape=(sm...]
where the time goes in v3:
time: 42.7 us; the launch traced here: 42.5 us
  Pallas kernels  38.3 us (90%)
  local copies, waits for them, and re-layouts  3.51 us (8%)
  between operations  0.67 us (2%)
    pallas_call x1, Pallas kernels, fused(): pl.pallas_call(functools.partial(kernel, kvecs, prefactor), out_shape=(sm...  38.3 us
    unnamed x16, local copies, waits for them, and re-layouts  3.51 us

profile of v3, /device:TPU:0, one launch (start us, length us, event | category | flops | bytes accessed | tf_op | source)
XLA Modules:
  0.0 42.5 jit_solution(7463614040740714076)
XLA Ops:
  0.6 0.0 copy-start.5
  0.6 0.7 %copy.9.pos_ref = f32[2,3,128]{2,1,0:T(4,128)S(1)} copy(f32[2,3,128]{2,0,1:T(2,128)} %param.7) | data formatting | bytes 6144 | tf_op args[0]
  1.3 0.0 copy-done.5
  1.3 0.0 copy-start.1
  1.3 0.0 copy-start.2
  1.3 0.0 copy-start.3
  1.3 0.0 copy-start.4
  1.4 0.1 copy.10.kint_ref
  1.5 0.5 %copy-done.1 = f32[3,128]{1,0:T(4,128)S(1)} copy-done((f32[3,128]{1,0:T(4,128)S(1)}, f32[3,128]{1,0:T(4,128)}, u32[]{:S(2)}) %copy-start.1) | copy-done | bytes 1560
  2.0 0.0 copy-done.2
  2.0 0.0 copy-done.3
  2.0 0.0 copy-done.4
  2.0 0.0 copy-start
  2.0 1.0 %copy-done = f32[128,640]{1,0:T(8,128)S(1)} copy-done((f32[128,640]{1,0:T(8,128)S(1)}, f32[128,640]{1,0:T(8,128)}, u32[]{:S(2)}) %copy-start) | copy-done | bytes 327704
  3.0 38.3 %shard_map.86 = (f32[3,128]{1,0:T(4,128)S(1)}, f32[3,128]{1,0:T(4,128)S(1)}) custom-call(f32[2,3,128]{2,1,0:T(4,128)S(1)} %copy.9.pos_ref, f32[128,640]{1,0:T(8,128)S(1)} %copy-done, f32[3,128]{1,0:T(4,128)S(1)} %copy-done.1, f32[3,128]{1,0:T(4,128)S(1)} %copy-done.2, s32[1,128]{1,0:T(1,128)S(1)} %bitcast.1, f32[6]{0:T(128)S(1)} %copy-done.4, ...), custom_call_target="tpu_custom_call" | custom-call | tf_op jit(solution)/shard_map/pallas_call | solution.py:587
  41.3 0.6 %copy.13 = f32[3,128]{1,0:T(4,128)} copy(f32[3,128]{1,0:T(4,128)S(1)} %get-tuple-element.4) | data formatting | bytes 3072
  41.9 0.6 %copy.14 = f32[3,128]{1,0:T(4,128)} copy(f32[3,128]{1,0:T(4,128)S(1)} %get-tuple-element.5) | data formatting | bytes 3072
Async XLA Ops:
  0.6 0.7 %copy-start.5 = (s32[384,3]{0,1:T(4,128)S(1)}, s32[384,3]{0,1:T(4,128)}, u32[]{:S(2)}) copy-start(s32[384,3]{0,1:T(4,128)} %param.13) | copy-start | bytes 13828
  1.3 0.7 %copy-start.1 = (f32[3,128]{1,0:T(4,128)S(1)}, f32[3,128]{1,0:T(4,128)}, u32[]{:S(2)}) copy-start(f32[3,128]{1,0:T(4,128)} %adj_ref.1) | copy-start | bytes 4612
  1.3 0.7 %copy-start.2 = (f32[3,128]{1,0:T(4,128)S(1)}, f32[3,128]{1,0:T(4,128)}, u32[]{:S(2)}) copy-start(f32[3,128]{1,0:T(4,128)} %fma_ref.1) | copy-start | bytes 4612
  1.3 0.7 %copy-start.3 = (s32[128]{0:T(128)S(1)}, s32[128]{0:T(128)}, u32[]{:S(2)}) copy-start(s32[128]{0:T(128)} %param.11) | copy-start | bytes 1540
  1.3 0.7 %copy-start.4 = (f32[6]{0:T(128)S(1)}, f32[6]{0:T(128)}, u32[]{:S(2)}) copy-start(f32[6]{0:T(128)} %mass_ref.1) | copy-start | bytes 76
  2.0 1.0 %copy-start = (f32[128,640]{1,0:T(8,128)S(1)}, f32[128,640]{1,0:T(8,128)}, u32[]{:S(2)}) copy-start(f32[128,640]{1,0:T(8,128)} %mom_hbm.1) | copy-start | bytes 983044

commit v4 on v3

--- a/solution.py
+++ b/solution.py
@@ -419,23 +419,25 @@
         both = jnp.concatenate([operand(*first), operand(*second)], axis=0)
         proj[...] = jnp.dot(both, w2[...], preferred_element_type=F32)
 
+    span = 32
+
     def factor_part(step, slot):
         acc[3:9] = jnp.zeros((6, 8, atoms), F32)
         real, imag = sums[slot, 0], sums[slot, 1]
         project((real, imag), (imag, -real))
 
-        @pl.loop(0, kdev // tile)
+        @pl.loop(0, kdev // span)
         def _(chunk):
-            at = pl.multiple_of(chunk * tile, tile)
+            at = pl.multiple_of(chunk * span, span)
             value = (
-                trig[step, 0, pl.ds(at, tile)] * proj[pl.ds(at, tile)]
-                + trig[step, 1, pl.ds(at, tile)] * proj[pl.ds(pl.multiple_of(kdev + at, tile), tile)]
+                trig[step, 0, pl.ds(at, span)] * proj[pl.ds(at, span)]
+                + trig[step, 1, pl.ds(at, span)] * proj[pl.ds(pl.multiple_of(kdev + at, span), span)]
             )
             row = 3
             for axis in range(3):
-                weighted = wide(kmap[3 + axis, pl.ds(at, tile)], GROUP) * value
+                weighted = wide(kmap[3 + axis, pl.ds(at, span)], GROUP) * value
                 for other in range(axis, 3):
-                    acc[row] += fold(wide(kmap[other, pl.ds(at, tile)], GROUP) * weighted)
+                    acc[row] += fold(wide(kmap[other, pl.ds(at, span)], GROUP) * weighted)
                     row += 1
 
     def tangent_part(step, slot):
@@ -443,15 +445,15 @@
         real, imag = sums[slot, 0], sums[slot, 1]
         project((real, imag), (-imag, real))
 
-        @pl.loop(0, kdev // tile)
+        @pl.loop(0, kdev // span)
         def _(chunk):
-            at = pl.multiple_of(chunk * tile, tile)
+            at = pl.multiple_of(chunk * span, span)
             value = (
-                trig[step, 0, pl.ds(at, tile)] * proj[pl.ds(at, tile)]
-                - trig[step, 1, pl.ds(at, tile)] * proj[pl.ds(pl.multiple_of(kdev + at, tile), tile)]
+                trig[step, 0, pl.ds(at, span)] * proj[pl.ds(at, span)]
+                - trig[step, 1, pl.ds(at, span)] * proj[pl.ds(pl.multiple_of(kdev + at, span), span)]
             )
             for axis in range(3):
-                acc[axis] += fold(wide(kmap[3 + axis, pl.ds(at, tile)], GROUP) * value)
+                acc[axis] += fold(wide(kmap[3 + axis, pl.ds(at, span)], GROUP) * value)
 
     def send_force(step, direction):
         summed = [jnp.sum(acc[row], axis=0, keepdims=True) for row in range(9)]

time: 42.7 us -> 42.6 us (level)
  no operation moved by 1% of the time
where the time goes in v4:
time: 42.6 us; the launch traced here: 42.4 us
  Pallas kernels  38.2 us (90%)
  local copies, waits for them, and re-layouts  3.51 us (8%)
  between operations  0.67 us (2%)
    pallas_call x1, Pallas kernels, fused(): pl.pallas_call(functools.partial(kernel, kvecs, prefactor), out_shape=(sm...  38.2 us
    unnamed x16, local copies, waits for them, and re-layouts  3.51 us

profile of v4, /device:TPU:0, one launch (start us, length us, event | category | flops | bytes accessed | tf_op | source)
XLA Modules:
  0.0 42.4 jit_solution(11511753166338736089)
XLA Ops:
  0.6 0.0 copy-start.5
  0.6 0.7 %copy.9.pos_ref = f32[2,3,128]{2,1,0:T(4,128)S(1)} copy(f32[2,3,128]{2,0,1:T(2,128)} %param.7) | data formatting | bytes 6144 | tf_op args[0]
  1.3 0.0 copy-done.5
  1.3 0.0 copy-start.1
  1.3 0.0 copy-start.2
  1.3 0.0 copy-start.3
  1.3 0.0 copy-start.4
  1.4 0.1 copy.10.kint_ref
  1.5 0.5 %copy-done.1 = f32[3,128]{1,0:T(4,128)S(1)} copy-done((f32[3,128]{1,0:T(4,128)S(1)}, f32[3,128]{1,0:T(4,128)}, u32[]{:S(2)}) %copy-start.1) | copy-done | bytes 1560
  2.0 0.0 copy-done.2
  2.0 0.0 copy-done.3
  2.0 0.0 copy-done.4
  2.0 0.0 copy-start
  2.0 1.0 %copy-done = f32[128,640]{1,0:T(8,128)S(1)} copy-done((f32[128,640]{1,0:T(8,128)S(1)}, f32[128,640]{1,0:T(8,128)}, u32[]{:S(2)}) %copy-start) | copy-done | bytes 327704
  3.0 38.2 %shard_map.86 = (f32[3,128]{1,0:T(4,128)S(1)}, f32[3,128]{1,0:T(4,128)S(1)}) custom-call(f32[2,3,128]{2,1,0:T(4,128)S(1)} %copy.9.pos_ref, f32[128,640]{1,0:T(8,128)S(1)} %copy-done, f32[3,128]{1,0:T(4,128)S(1)} %copy-done.1, f32[3,128]{1,0:T(4,128)S(1)} %copy-done.2, s32[1,128]{1,0:T(1,128)S(1)} %bitcast.1, f32[6]{0:T(128)S(1)} %copy-done.4, ...), custom_call_target="tpu_custom_call" | custom-call | tf_op jit(solution)/shard_map/pallas_call | solution.py:589
  41.2 0.6 %copy.13 = f32[3,128]{1,0:T(4,128)} copy(f32[3,128]{1,0:T(4,128)S(1)} %get-tuple-element.4) | data formatting | bytes 3072
  41.8 0.6 %copy.14 = f32[3,128]{1,0:T(4,128)} copy(f32[3,128]{1,0:T(4,128)S(1)} %get-tuple-element.5) | data formatting | bytes 3072
Async XLA Ops:
  0.6 0.7 %copy-start.5 = (s32[384,3]{0,1:T(4,128)S(1)}, s32[384,3]{0,1:T(4,128)}, u32[]{:S(2)}) copy-start(s32[384,3]{0,1:T(4,128)} %param.13) | copy-start | bytes 13828
  1.3 0.7 %copy-start.1 = (f32[3,128]{1,0:T(4,128)S(1)}, f32[3,128]{1,0:T(4,128)}, u32[]{:S(2)}) copy-start(f32[3,128]{1,0:T(4,128)} %adj_ref.1) | copy-start | bytes 4612
  1.3 0.7 %copy-start.2 = (f32[3,128]{1,0:T(4,128)S(1)}, f32[3,128]{1,0:T(4,128)}, u32[]{:S(2)}) copy-start(f32[3,128]{1,0:T(4,128)} %fma_ref.1) | copy-start | bytes 4612
  1.3 0.7 %copy-start.3 = (s32[128]{0:T(128)S(1)}, s32[128]{0:T(128)}, u32[]{:S(2)}) copy-start(s32[128]{0:T(128)} %param.11) | copy-start | bytes 1540
  1.3 0.7 %copy-start.4 = (f32[6]{0:T(128)S(1)}, f32[6]{0:T(128)}, u32[]{:S(2)}) copy-start(f32[6]{0:T(128)} %mass_ref.1) | copy-start | bytes 76
  2.0 1.0 %copy-start = (f32[128,640]{1,0:T(8,128)S(1)}, f32[128,640]{1,0:T(8,128)}, u32[]{:S(2)}) copy-start(f32[128,640]{1,0:T(8,128)} %mom_hbm.1) | copy-start | bytes 983044
